TPU v7x, 256 devices: a whole 4x4x8 slice. The times are simulated.
256 devices in a mesh: replica: 16 (over z, core), mp: 16 (over y, x).
Axes of the slice: x: 4, y: 4, z: 8, core: 2. Of those that a mesh axis runs over, the one named last changes fastest.
Arguments:
- gradients: bfloat16 [16, 8, 768, 3072], P('replica', None, 'mp'), may hold values from -6 to 6
- feedback: bfloat16 [16, 8, 768, 3072], P('replica', None, 'mp'), may hold values from -4 to 4
- right_init: bfloat16 [8, 3072, 32], replicated, may hold values from -0.109375 to 0.109375
- gram_root: float32 [8, 32, 32], replicated, as said below
- owners: int32 [8], replicated, may hold values from 0 to 15, as said below
- momentum: float32 [16, 1, 768, 3072], P('mp', None, 'replica'), may hold values from -4 to 4
- master_weights: float32 [16, 1, 768, 3072], P('mp', None, 'replica'), may hold values from -1.5 to 1.5
- vector_grads: float32 [16, 10752], P('replica', 'mp'), may hold values from -6 to 6
- vector_momentum: float32 [10752], P('mp'), may hold values from -6 to 6
- vector_params: float32 [10752], P('mp'), may hold values from -6 to 6
Outputs:
- new_feedback: bfloat16 [16, 8, 768, 3072], P('replica', None, 'mp')
- new_momentum: float32 [16, 1, 768, 3072], P('mp', None, 'replica')
- new_master: float32 [16, 1, 768, 3072], P('mp', None, 'replica')
- new_weights: bfloat16 [8, 768, 3072], P(None, 'replica')
- new_vector_momentum: float32 [10752], P('mp')
- new_vector_params: float32 [10752], P('mp')
Inputs may be any that keep to these rules, and one draw needn't show every extreme that they name: `owners`: every matrix has one owner; no owner holds more than 1 of the 8 matrices, and one owner holds exactly 1. `gram_root`: each matrix is the identity plus off-diagonal terms, times a positive scale.
All inputs are finite; a program needn't handle non-finite values.
Results may differ from a plain program's by a relative error of at most 0.007.
Values may be sent and summed in bfloat16 or wider, within the bound.
A program may use at most 192 MiB of HBM per device.

v0:
```python
import jax
import jax.numpy as jnp
from jax import lax
from jax.sharding import PartitionSpec as P


def per_device(
    gradients,
    feedback,
    right_init,
    gram_root,
    owners,
    momentum,
    master_weights,
    vector_grads,
    vector_momentum,
    vector_params,
):
    highest = lax.Precision.HIGHEST
    compensated = (gradients[0].astype(jnp.float32) + feedback[0].astype(jnp.float32)).astype(
        jnp.bfloat16
    )
    owner_count = lax.axis_size("mp")
    capacity = momentum.shape[1]
    matrices = owners.shape[0]
    replica_rows = momentum.shape[2]
    mp_index = lax.axis_index("mp")
    replica_index = lax.axis_index("replica")
    same_owner = owners[:, None] == owners[None, :]
    earlier = jnp.arange(matrices)[:, None] < jnp.arange(matrices)[None, :]
    ranks = jnp.sum((same_owner & earlier).astype(jnp.int32), axis=0)
    slots = owners * capacity + ranks
    slot_table = (slots[None, :] == jnp.arange(owner_count * capacity)[:, None]).astype(jnp.float32)
    table_narrow = slot_table.astype(jnp.bfloat16)
    table_mine = lax.dynamic_slice_in_dim(slot_table, mp_index * capacity, capacity, 0)
    left_terms = jnp.einsum(
        "kmn,knr->kmr", compensated, right_init, preferred_element_type=jnp.float32
    )
    left_sum = lax.psum(left_terms, "replica")
    left_rows = jnp.einsum("kmr,krs->kms", left_sum, gram_root, precision=highest).astype(
        jnp.bfloat16
    )
    right_terms = jnp.einsum(
        "kmn,kms->kns", compensated, left_rows, preferred_element_type=jnp.float32
    )
    right_new = lax.psum(right_terms, ("replica", "mp"))
    left_all = lax.all_gather(left_rows, "mp", axis=1, tiled=True)
    approx_rows = jnp.einsum(
        "kms,kns->kmn", left_rows.astype(jnp.float32), right_new, precision=highest
    )
    new_feedback = (compensated.astype(jnp.float32) - approx_rows).astype(jnp.bfloat16)
    left_chosen = jnp.einsum(
        "ck,kmr->cmr", table_mine.astype(jnp.bfloat16), left_all, preferred_element_type=jnp.float32
    )
    left_chosen = lax.dynamic_slice_in_dim(
        left_chosen, replica_index * replica_rows, replica_rows, 1
    )
    right_chosen = jnp.einsum("ck,knr->cnr", table_mine, right_new, precision=highest)
    approx_slots = jnp.einsum("cmr,cnr->cmn", left_chosen, right_chosen, precision=highest)
    new_momentum = 0.9 * momentum[0] + approx_slots
    new_master = master_weights[0] - 0.1 * new_momentum
    master_narrow = new_master.astype(jnp.bfloat16)
    weight_slots = lax.all_gather(master_narrow, "mp", axis=0, tiled=True)
    new_weights = jnp.einsum(
        "sk,smn->kmn", table_narrow, weight_slots, preferred_element_type=jnp.float32
    ).astype(jnp.bfloat16)
    vector_total = lax.psum(vector_grads[0], "replica")
    new_vector_momentum = 0.9 * vector_momentum + vector_total
    new_vector_params = vector_params - 0.1 * new_vector_momentum
    return (
        new_feedback[None],
        new_momentum[None],
        new_master[None],
        new_weights,
        new_vector_momentum,
        new_vector_params,
    )


def solution(mesh):
    return jax.shard_map(
        per_device,
        mesh=mesh,
        in_specs=(
            P("replica", None, "mp", None),
            P("replica", None, "mp", None),
            P(),
            P(),
            P(),
            P("mp", None, "replica", None),
            P("mp", None, "replica", None),
            P("replica", "mp"),
            P("mp"),
            P("mp"),
        ),
        out_specs=(
            P("replica", None, "mp", None),
            P("mp", None, "replica", None),
            P("mp", None, "replica", None),
            P(None, "replica", None),
            P("mp"),
            P("mp"),
        ),
        check_vma=False,
    )
```

profile of v0, /device:TPU:1, one launch (start us, length us, event | category | flops | bytes accessed | tf_op | source)
XLA Modules:
  0.0 481.2 jit_solution(16211220204946410669)
XLA Ops:
  7.2 0.0 copy-start
  7.2 0.0 all-reduce.3.cloned.1.call-start
  7.2 0.8 reduce.1
  8.0 0.6 copy-done
  8.6 0.0 copy-start.5
  8.6 3.1 fusion.27
  11.8 50.5 %all-reduce = (f32[8,48,32]{1,2,0:T(8,128)S(1)}, f32[672]{0:T(1024)S(1)}) all-reduce(f32[8,48,32]{1,2,0:T(8,128)S(1)} %fusion.27, f32[672]{0:T(1024)S(1)} %reduce.1), channel_id=1, replica_groups=mesh['replica'=16,'mp'=16] {'replica'}, use_global_device_ids=true, to_apply=%region_0.0 | all-reduce | flops 12960 | bytes 103680 | tf_op jit(solution)/shard_map/psum | solution.py:39
  62.2 0.0 copy-done.5
  62.3 0.4 convolution_convert_fusion
  62.6 4.7 fusion.25
  67.3 0.0 copy-start.8
  67.3 0.0 all-reduce.3.cloned.1.call-update
  67.4 0.0 all-gather.3.cloned.1.call-start
  67.4 0.1 copy.26
  67.6 0.4 copy-done.8
  68.0 0.1 convert_reduce_fusion
  68.1 22.7 %all_gather.6 = bf16[8,768,32]{2,0,1:T(8,128)(2,1)S(1)} all-gather(bf16[8,48,32]{2,0,1:T(8,128)(2,1)S(1)} %copy.26), channel_id=1, replica_groups=mesh['replica'=16,'mp'=16] {'mp'}, dimensions={1}, use_global_device_ids=true | all-gather | bytes 417792 | tf_op jit(solution)/shard_map/all_gather | solution.py:47
  90.8 1.1 multiply_reduce_fusion
  91.9 239.2 %all-reduce.3.cloned.1.call-done = f32[8,3072,32]{1,2,0:T(8,128)} async-done(((f32[8,3072,32]{1,2,0:T(8,128)}), f32[8,3072,32]{1,2,0:T(8,128)}) %all-reduce.3.cloned.1.call-update) | async-done | bytes 3145744 | tf_op jit(solution)/shard_map/psum | solution.py:46
  331.1 44.7 %fusion.6 = f32[1,3072,32]{0,1,2:T(8,128)} fusion(f32[8,3072,32]{1,2,0:T(8,128)} %all-reduce.3.cloned.1.call-done, pred[16,8]{1,0:T(8,128)(4,1)S(1)} %get-tuple-element.31, s32[]{:T(128)S(6)} %select_n.6), kind=kOutput, calls=%fused_computation.7 | convolution fusion | flops 9437184 | bytes 3539460 | tf_op jit(solution)/shard_map/ck,knr->cnr/dot_general | solution.py:58
  375.7 0.0 copy-start.3
  375.7 0.0 copy-start.4
  375.7 27.1 %copy.35 = f32[1,3072,32]{1,2,0:T(8,128)S(1)} copy(f32[1,3072,32]{0,1,2:T(8,128)} %fusion.6) | data formatting | bytes 786432 | tf_op jit(solution)/shard_map/ck,knr->cnr/dot_general | solution.py:58
  402.9 0.0 copy-done.3
  402.9 0.0 copy-start.6
  402.9 0.0 copy-start.7
  402.9 0.6 convolution_add_fusion
  403.6 0.0 copy-done.4
  403.6 0.0 copy-start.2
  403.6 1.2 fusion.10
  404.7 0.0 all-gather.3.cloned.1.call-update
  404.8 0.0 copy-done.6
  404.8 0.0 copy-done.7
  404.8 0.6 multiply_subtract_fusion
  405.4 7.4 %fusion.5 = bf16[1,8,48,3072]{3,2,1,0:T(8,128)(2,1)} fusion(bf16[8,48,32]{1,2,0:T(8,128)(2,1)S(1)} %convolution_convert_fusion, f32[8,3072,32]{1,2,0:T(8,128)} %all-reduce.3.cloned.1.call-done, bf16[1,8,48,3072]{3,2,1,0:T(8,128)(2,1)} %param.11, bf16[1,8,48,3072]{3,2,1,0:T(8,128)(2,1)} %param.10), kind=kOutput, calls=%fused_computation.5 | convolution fusion | flops 461242368 | bytes 10248192 | tf_op jit(solution)/shard_map/kms,kns->kmn/dot_general | solution.py:48
  412.8 0.0 copy-done.2
  412.8 51.4 %all-gather.3.cloned.1.call-done = bf16[768,3072]{1,0:T(8,128)(2,1)} async-done(((bf16[48,3072]{1,0:T(8,128)(2,1)}), bf16[768,3072]{1,0:T(8,128)(2,1)}) %all-gather.3.cloned.1.call-update) | async-done | bytes 4718608 | tf_op jit(solution)/shard_map/all_gather | solution.py:63
  464.2 0.0 copy-start.1
  464.2 7.5 %fusion.2 = bf16[8,48,3072]{2,0,1:T(8,128)(2,1)S(1)} fusion(bf16[16,48,3072]{2,1,0:T(8,128)(2,1)} %bitcast.41, s32[8]{0:T(128)S(1)} %add.27), kind=kOutput, calls=%fused_computation.4 | convolution fusion | flops 38928768 | bytes 7077920 | tf_op jit(solution)/shard_map/sk,smn->kmn/dot_general | solution.py:64
  471.7 2.7 copy.29
  474.4 0.0 copy-done.1
  (3 shorter events, 0.0 us)
Async XLA Ops:
  7.2 1.4 copy-start
  7.2 323.9 %all-reduce.3.cloned.1.call-start = ((), (), s32[]{:S(2)}) async-start(), calls=%async_computation | async-start | bytes 6291456 | tf_op jit(solution)/shard_map/psum | solution.py:46
  8.6 53.6 %copy-start.5 = (f32[8,32,32]{2,1,0:T(8,128)S(1)}, f32[8,32,32]{2,1,0:T(8,128)}, u32[]{:S(2)}) copy-start(f32[8,32,32]{2,1,0:T(8,128)} %param.13) | copy-start | bytes 98308
  67.3 0.7 copy-start.8
  67.4 396.9 %all-gather.3.cloned.1.call-start = ((), (), s32[]{:S(2)}) async-start(), calls=%async_computation.1 | async-start | bytes 5013504 | tf_op jit(solution)/shard_map/all_gather | solution.py:63
  375.7 27.1 %copy-start.3 = (f32[1,1,48,3072]{3,2,1,0:T(8,128)S(1)}, f32[1,1,48,3072]{3,2,1,0:T(8,128)}, u32[]{:S(2)}) copy-start(f32[1,1,48,3072]{3,2,1,0:T(8,128)} %param.15) | copy-start | bytes 1769476
  375.7 27.8 %copy-start.4 = (f32[1,1,48,3072]{3,2,1,0:T(8,128)S(1)}, f32[1,1,48,3072]{3,2,1,0:T(8,128)}, u32[]{:S(2)}) copy-start(f32[1,1,48,3072]{3,2,1,0:T(8,128)} %param.16) | copy-start | bytes 1769476
  402.9 1.9 copy-start.6
  402.9 1.9 copy-start.7
  403.6 9.2 %copy-start.2 = (f32[48,3072]{1,0:T(8,128)}, f32[48,3072]{1,0:T(8,128)S(1)}, u32[]{:S(2)}) copy-start(f32[48,3072]{1,0:T(8,128)S(1)} %convolution_add_fusion) | copy-start | bytes 1769476
  464.2 10.2 %copy-start.1 = (bf16[8,3072,32]{1,2,0:T(8,128)(2,1)S(1)}, bf16[8,3072,32]{1,2,0:T(8,128)(2,1)}, u32[]{:S(2)}) copy-start(bf16[8,3072,32]{1,2,0:T(8,128)(2,1)} %param.12) | copy-start | bytes 4718596
Sparse Core Ops, SparseCore 0:
  67.5 263.5 all-reduce.2
  404.9 59.2 all-gather.2
where the time goes:
time: 482 us; the launch traced here: 481 us
  waiting for transfers between devices  291 us (60%)
  blocking collectives  73.2 us (15%)
  matrix products  68.4 us (14%)
  local copies, waits for them, and re-layouts  31 us (6%)
  between operations  14.2 us (3%)
    psum x1, waiting for transfers between devices, per_device(): right_new = lax.psum(right_terms, ('replica', 'mp'))  239 us
    all_gather x1, waiting for transfers between devices, per_device(): weight_slots = lax.all_gather(master_narrow, 'mp', axis=0, tiled=True)  51.4 us
    psum x1, blocking collectives, per_device(): left_sum = lax.psum(left_terms, 'replica')  50.5 us
    dot_general x1, matrix products, per_device(): jnp.einsum('ck,knr->cnr', table_mine, right_new, precision=highest)  44.7 us
    dot_general x1, local copies, waits for them, and re-layouts, per_device(): jnp.einsum('ck,knr->cnr', table_mine, right_new, precision=highest)  27.1 us
    all_gather x1, blocking collectives, per_device(): left_all = lax.all_gather(left_rows, 'mp', axis=1, tiled=True)  22.7 us
  transfers between devices with their start and end apart: 2, of which 2 were waited for; matrix products, arithmetic and copies ran while one was open for 2% of the time, Pallas kernels for 0%

commit v1 on v0

--- a/solution.py
+++ b/solution.py
@@ -60,7 +60,15 @@
     new_momentum = 0.9 * momentum[0] + approx_slots
     new_master = master_weights[0] - 0.1 * new_momentum
     master_narrow = new_master.astype(jnp.bfloat16)
-    weight_slots = lax.all_gather(master_narrow, "mp", axis=0, tiled=True)
+    weight_slots = jnp.concatenate(
+        lax.all_to_all(
+            jnp.stack([master_narrow] * lax.axis_size("mp"), axis=0),
+            concat_axis=0,
+            split_axis=0,
+            axis_name="mp",
+        ),
+        axis=0,
+    )
     new_weights = jnp.einsum(
         "sk,smn->kmn", table_narrow, weight_slots, preferred_element_type=jnp.float32
     ).astype(jnp.bfloat16)

time: 482 us -> 504 us (1.046); the launches traced: 481 us -> 498 us
  waiting for transfers between devices: 291 us -> 298 us
  starting transfers between devices: 0.08 us -> 6.64 us
    all_to_all x0 -> x1, waiting for transfers between devices: none -> 58.8 us  [per_device(): lax.all_to_all(jnp.stack([master_narrow] * lax.axis_size('mp'), axis=0),...]
    all_gather x1 -> x0, waiting for transfers between devices: 51.4 us -> none  [per_device(): weight_slots = lax.all_gather(master_narrow, 'mp', axis=0, tiled=True)]
    all_to_all x0 -> x1, starting transfers between devices: none -> 6.6 us  [per_device(): lax.all_to_all(jnp.stack([master_narrow] * lax.axis_size('mp'), axis=0),...]
where the time goes in v1:
time: 504 us; the launch traced here: 498 us
  waiting for transfers between devices  298 us (59%)
  blocking collectives  73.4 us (15%)
  matrix products  68.5 us (14%)
  local copies, waits for them, and re-layouts  33.8 us (7%)
  between operations  14.2 us (3%)
  starting transfers between devices  6.64 us (1%)
    psum x1, waiting for transfers between devices, per_device(): right_new = lax.psum(right_terms, ('replica', 'mp'))  239 us
    all_to_all x1, waiting for transfers between devices, per_device(): lax.all_to_all(jnp.stack([master_narrow] * lax.axis_size('mp'), axis=0),...  58.8 us
    psum x1, blocking collectives, per_device(): left_sum = lax.psum(left_terms, 'replica')  50.5 us
    dot_general x1, matrix products, per_device(): jnp.einsum('ck,knr->cnr', table_mine, right_new, precision=highest)  44.7 us
    dot_general x1, local copies, waits for them, and re-layouts, per_device(): jnp.einsum('ck,knr->cnr', table_mine, right_new, precision=highest)  27.1 us
    all_gather x1, blocking collectives, per_device(): left_all = lax.all_gather(left_rows, 'mp', axis=1, tiled=True)  23 us
  transfers between devices with their start and end apart: 2, of which 2 were waited for; matrix products, arithmetic and copies ran while one was open for 2% of the time, Pallas kernels for 0%

profile of v1, /device:TPU:1, one launch (start us, length us, event | category | flops | bytes accessed | tf_op | source)
XLA Modules:
  0.0 497.9 jit_solution(1466325815826389391)
XLA Ops:
  7.2 0.0 copy-start
  7.2 0.0 all-reduce.3.cloned.1.call-start
  7.2 0.8 reduce.1
  8.0 0.6 copy-done
  8.6 0.0 copy-start.5
  8.6 3.1 fusion.28
  11.8 50.5 %all-reduce = (f32[8,48,32]{1,2,0:T(8,128)S(1)}, f32[672]{0:T(1024)S(1)}) all-reduce(f32[8,48,32]{1,2,0:T(8,128)S(1)} %fusion.28, f32[672]{0:T(1024)S(1)} %reduce.1), channel_id=1, replica_groups=mesh['replica'=16,'mp'=16] {'replica'}, use_global_device_ids=true, to_apply=%region_0.0 | all-reduce | flops 12960 | bytes 103680 | tf_op jit(solution)/shard_map/psum | solution.py:39
  62.2 0.0 copy-done.5
  62.3 0.4 convolution_convert_fusion
  62.6 4.7 fusion.26
  67.4 0.0 copy-start.8
  67.4 0.0 all-reduce.3.cloned.1.call-update
  67.4 0.1 copy.25
  67.5 0.5 copy-done.8
  68.0 0.1 convert_reduce_fusion
  68.1 23.0 %all_gather.3 = bf16[8,768,32]{2,0,1:T(8,128)(2,1)S(1)} all-gather(bf16[8,48,32]{2,0,1:T(8,128)(2,1)S(1)} %copy.25), channel_id=1, replica_groups=mesh['replica'=16,'mp'=16] {'mp'}, dimensions={1}, use_global_device_ids=true | all-gather | bytes 417792 | tf_op jit(solution)/shard_map/all_gather | solution.py:47
  91.1 1.1 multiply_reduce_fusion
  92.2 238.8 %all-reduce.3.cloned.1.call-done = f32[8,3072,32]{1,2,0:T(8,128)} async-done(((f32[8,3072,32]{1,2,0:T(8,128)}), f32[8,3072,32]{1,2,0:T(8,128)}) %all-reduce.3.cloned.1.call-update) | async-done | bytes 3145744 | tf_op jit(solution)/shard_map/psum | solution.py:46
  331.0 44.7 %fusion.7 = f32[1,3072,32]{0,1,2:T(8,128)} fusion(f32[8,3072,32]{1,2,0:T(8,128)} %all-reduce.3.cloned.1.call-done, pred[16,8]{1,0:T(8,128)(4,1)S(1)} %get-tuple-element.31, s32[]{:T(128)S(6)} %select_n.6), kind=kOutput, calls=%fused_computation.8 | convolution fusion | flops 9437184 | bytes 3539460 | tf_op jit(solution)/shard_map/ck,knr->cnr/dot_general | solution.py:58
  375.8 0.0 copy-start.3
  375.8 0.0 copy-start.4
  375.8 27.1 %copy.34 = f32[1,3072,32]{1,2,0:T(8,128)S(1)} copy(f32[1,3072,32]{0,1,2:T(8,128)} %fusion.7) | data formatting | bytes 786432 | tf_op jit(solution)/shard_map/ck,knr->cnr/dot_general | solution.py:58
  402.9 0.0 copy-done.3
  402.9 0.6 convolution_add_fusion
  403.6 0.0 copy-done.4
  403.6 0.0 copy-start.2
  403.6 1.1 fusion.11
  404.6 2.8 stack.2
  407.4 0.0 copy-done.2
  407.4 0.0 copy-start.6
  407.4 0.0 copy-start.7
  407.4 6.6 %all-to-all-start = ((bf16[16,1,48,3072]{3,2,1,0:T(8,128)(2,1)}), bf16[16,1,48,3072]{3,2,1,0:T(8,128)(2,1)}, u32[]{:S(2)}, u32[]{:S(2)}) async-start(bf16[16,1,48,3072]{3,2,1,0:T(8,128)(2,1)} %stack.2), calls=%async_computation | async-start | bytes 9437184 | tf_op jit(solution)/shard_map/all_to_all | solution.py:64
  414.0 0.0 copy-done.6
  414.0 0.0 copy-done.7
  414.0 0.6 multiply_subtract_fusion
  414.6 7.4 %fusion.6 = bf16[1,8,48,3072]{3,2,1,0:T(8,128)(2,1)} fusion(bf16[8,48,32]{1,2,0:T(8,128)(2,1)S(1)} %convolution_convert_fusion, f32[8,3072,32]{1,2,0:T(8,128)} %all-reduce.3.cloned.1.call-done, bf16[1,8,48,3072]{3,2,1,0:T(8,128)(2,1)} %param.11, bf16[1,8,48,3072]{3,2,1,0:T(8,128)(2,1)} %param.10), kind=kOutput, calls=%fused_computation.6 | convolution fusion | flops 461242368 | bytes 10248192 | tf_op jit(solution)/shard_map/kms,kns->kmn/dot_general | solution.py:48
  422.0 58.8 %all-to-all-done = bf16[16,1,48,3072]{3,2,1,0:T(8,128)(2,1)} async-done(((bf16[16,1,48,3072]{3,2,1,0:T(8,128)(2,1)}), bf16[16,1,48,3072]{3,2,1,0:T(8,128)(2,1)}, u32[]{:S(2)}, u32[]{:S(2)}) %all-to-all-start) | async-done | bytes 4718624 | tf_op jit(solution)/shard_map/all_to_all | solution.py:64
  480.8 0.0 copy-start.1
  480.8 7.5 %fusion.3 = bf16[8,48,3072]{2,0,1:T(8,128)(2,1)S(1)} fusion(bf16[16,1,48,3072]{3,2,1,0:T(8,128)(2,1)} %all-to-all-done, s32[8]{0:T(128)S(1)} %add.27), kind=kOutput, calls=%fused_computation.5 | convolution fusion | flops 38928768 | bytes 7077920 | tf_op jit(solution)/shard_map/sk,smn->kmn/dot_general | solution.py:72
  488.3 2.7 copy.28
  491.0 0.0 copy-done.1
  (3 shorter events, 0.0 us)
Async XLA Ops:
  7.2 1.4 copy-start
  7.2 323.9 %all-reduce.3.cloned.1.call-start = ((), (), s32[]{:S(2)}) async-start(), calls=%async_computation.1 | async-start | bytes 6291456 | tf_op jit(solution)/shard_map/psum | solution.py:46
  8.6 53.6 %copy-start.5 = (f32[8,32,32]{2,1,0:T(8,128)S(1)}, f32[8,32,32]{2,1,0:T(8,128)}, u32[]{:S(2)}) copy-start(f32[8,32,32]{2,1,0:T(8,128)} %param.13) | copy-start | bytes 98308
  67.4 0.7 copy-start.8
  375.8 27.1 %copy-start.3 = (f32[1,1,48,3072]{3,2,1,0:T(8,128)S(1)}, f32[1,1,48,3072]{3,2,1,0:T(8,128)}, u32[]{:S(2)}) copy-start(f32[1,1,48,3072]{3,2,1,0:T(8,128)} %param.15) | copy-start | bytes 1769476
  375.8 27.8 %copy-start.4 = (f32[1,1,48,3072]{3,2,1,0:T(8,128)S(1)}, f32[1,1,48,3072]{3,2,1,0:T(8,128)}, u32[]{:S(2)}) copy-start(f32[1,1,48,3072]{3,2,1,0:T(8,128)} %param.16) | copy-start | bytes 1769476
  403.6 3.8 copy-start.2
  407.4 6.6 %copy-start.6 = (f32[672]{0:T(1024)S(1)}, f32[672]{0:T(1024)}, u32[]{:S(2)}) copy-start(f32[672]{0:T(1024)} %param.19) | copy-start | bytes 8068
  407.4 6.6 %copy-start.7 = (f32[672]{0:T(1024)S(1)}, f32[672]{0:T(1024)}, u32[]{:S(2)}) copy-start(f32[672]{0:T(1024)} %param.18) | copy-start | bytes 8068
  407.4 73.4 %all-to-all-start = ((bf16[16,1,48,3072]{3,2,1,0:T(8,128)(2,1)}), bf16[16,1,48,3072]{3,2,1,0:T(8,128)(2,1)}, u32[]{:S(2)}, u32[]{:S(2)}) async-start(bf16[16,1,48,3072]{3,2,1,0:T(8,128)(2,1)} %stack.2), calls=%async_computation | async-start | bytes 9437184 | tf_op jit(solution)/shard_map/all_to_all | solution.py:64
  480.8 10.2 %copy-start.1 = (bf16[8,3072,32]{1,2,0:T(8,128)(2,1)S(1)}, bf16[8,3072,32]{1,2,0:T(8,128)(2,1)}, u32[]{:S(2)}) copy-start(bf16[8,3072,32]{1,2,0:T(8,128)(2,1)} %param.12) | copy-start | bytes 4718596
Sparse Core Ops, SparseCore 0:
  67.5 263.4 all-reduce.2
